TPU v7x, 32 devices: a whole 2x2x4 slice. The times are simulated.
32 devices in a mesh: clip: 2 (over y), frame: 4 (over z), track: 4 (over x, core).
Axes of the slice: x: 2, y: 2, z: 4, core: 2. Of those that a mesh axis runs over, the one named last changes fastest.
Arguments:
- feature_maps: bfloat16 [8, 4096, 256], P(('clip', 'frame')), parts along dimension 0, may hold values from -6 to 6
- query_frame: int32 [1024], P('clip'), parts along dimension 0, may hold values from 0 to 3
- query_row: int32 [1024], P('clip'), parts along dimension 0, may hold values from 0 to 63
- query_col: int32 [1024], P('clip'), parts along dimension 0, may hold values from 0 to 63
- track_order: int32 [1024], P('clip'), parts along dimension 0, may hold values from 0 to 511, each once
- conv_weight: float32 [16, 9], replicated, may hold values from -2 to 2
- conv_bias: float32 [16], replicated, may hold values from -2 to 2
- head_weight: float32 [16], replicated, may hold values from -2 to 2
- mix_in: bfloat16 [256, 1024], replicated, may hold values from -0.375 to 0.375
- temporal_taps: float32 [3, 1024], replicated, may hold values from -2.5 to 2.5
- mix_gain: float32 [1024], replicated, may hold values from 0.25 to 1.75
- mix_out: bfloat16 [1024, 3], replicated, may hold values from -0.1875 to 0.1875
Outputs:
- estimates: float32 [1024, 3, 4], P(('clip', 'frame', 'track')), parts along dimension 0
There are 2 independent parts, one for each index of `clip`. A program takes and returns all parts, laid end to end along the dimension named above; an argument that names none is the same for every part. Nothing has to cross between parts.
Inputs may be any that keep to these rules, and one draw needn't show every extreme that they name: `track_order`: each track appears in exactly one slot.
All inputs are finite; a program needn't handle non-finite values.
Results may differ from a plain program's by a relative error of at most 0.0053.
Values may be sent and summed in bfloat16 or wider, within the bound.
No kernel may reach another device: no remote copies, remote signals or barrier semaphores. Data moves between devices by JAX's collectives and lax.ppermute only.
A program may use at most 64 MiB of HBM per device.

v0:
```python
import math
import jax
import jax.numpy as jnp
from jax import lax
from jax.sharding import PartitionSpec as P

GRID_H = 64
GRID_W = 64


def padded_2(block, sides, width):
    for axis, dim in sides:
        count = lax.axis_size(axis)
        forward = [(i, i + 1) for i in range(count - 1)]
        backward = [(target, source) for source, target in forward]
        low = lax.ppermute(
            lax.slice_in_dim(block, block.shape[dim] - width, None, axis=dim), axis, forward
        )
        high = lax.ppermute(lax.slice_in_dim(block, 0, width, axis=dim), axis, backward)
        block = jnp.concatenate([low, block, high], axis=dim)
    return block


def conv_logits(cost, conv_weight, conv_bias, head_weight):
    height, width = (cost.shape[1], cost.shape[2])
    padded = jnp.pad(cost, ((0, 0), (1, 1), (1, 1)))
    logit = jnp.zeros(cost.shape, jnp.float32)
    for channel in range(conv_weight.shape[0]):
        acc = jnp.zeros(cost.shape, jnp.float32) + conv_bias[channel]
        for tap in range(9):
            acc = (
                acc
                + conv_weight[channel, tap]
                * padded[:, tap // 3 : tap // 3 + height, tap % 3 : tap % 3 + width]
            )
        logit = logit + head_weight[channel] * jax.nn.relu(acc)
    return logit


def block_terms(qblock, maps, conv_weight, conv_bias, head_weight, row_pos, col_pos):
    cost = lax.dot_general(
        qblock, maps, (((1,), (1,)), ((), ())), preferred_element_type=jnp.float32
    )
    cost = cost * (1.0 / math.sqrt(maps.shape[1]))
    logit = conv_logits(
        cost.reshape(cost.shape[0], GRID_H, GRID_W), conv_weight, conv_bias, head_weight
    )
    heat = jax.nn.softmax(logit.reshape(cost.shape), axis=-1)
    row_est = jnp.sum(heat * row_pos, axis=-1).astype(jnp.bfloat16)
    col_est = jnp.sum(heat * col_pos, axis=-1).astype(jnp.bfloat16)
    sampled = jnp.dot(heat.astype(jnp.bfloat16), maps, preferred_element_type=jnp.float32).astype(
        jnp.bfloat16
    )
    return (sampled, row_est, col_est)


def temporal_mix(extended, temporal_taps, mix_gain, mix_out):
    mixed = (
        temporal_taps[0] * extended[:, :-2]
        + temporal_taps[1] * extended[:, 1:-1]
        + temporal_taps[2] * extended[:, 2:]
    )
    normed = mixed * lax.rsqrt(jnp.mean(mixed * mixed, axis=-1, keepdims=True) + 1e-06) * mix_gain
    hidden = jax.nn.gelu(normed).astype(jnp.bfloat16)
    rows, frames_here = (hidden.shape[0], hidden.shape[1])
    delta = jnp.dot(
        hidden.reshape(rows * frames_here, hidden.shape[2]),
        mix_out,
        preferred_element_type=jnp.float32,
    )
    return delta.reshape(rows, frames_here, 3)


def assemble(row_est, col_est, delta):
    return jnp.stack(
        [
            row_est.astype(jnp.float32) + delta[:, :, 0],
            col_est.astype(jnp.float32) + delta[:, :, 1],
            delta[:, :, 2],
        ],
        axis=1,
    )


def project(sampled, mix_in):
    rows, frames_here, chan = sampled.shape
    projected = jnp.dot(
        sampled.reshape(rows * frames_here, chan), mix_in, preferred_element_type=jnp.float32
    )
    return projected.reshape(rows, frames_here, mix_in.shape[1])


def on_device(
    feature_maps,
    query_frame,
    query_row,
    query_col,
    track_order,
    conv_weight,
    conv_bias,
    head_weight,
    mix_in,
    temporal_taps,
    mix_gain,
    mix_out,
):
    frame_count = lax.axis_size("frame")
    track_count = lax.axis_size("track")
    frame_here = lax.axis_index("frame")
    track_here = lax.axis_index("track")
    f_dev, pixels, chan = feature_maps.shape
    total = track_order.shape[0]
    tr_dev = total // track_count
    sub_rows = tr_dev // frame_count
    slots = (
        jnp.arange(frame_count, dtype=jnp.int32)[:, None] * track_count + track_here
    ) * sub_rows
    slots = (slots + jnp.arange(sub_rows, dtype=jnp.int32)[None, :]).reshape(tr_dev)
    tracks = track_order[slots]
    local_frame = query_frame[tracks] - frame_here * f_dev
    owned = (local_frame >= 0) & (local_frame < f_dev)
    pixel_ids = query_row[tracks] * GRID_W + query_col[tracks]
    flat = jnp.clip(local_frame, 0, f_dev - 1) * pixels + pixel_ids
    picks = feature_maps.reshape(f_dev * pixels, chan)[flat]
    partial_value = jnp.where(owned[:, None], picks, jnp.zeros((), picks.dtype))
    queries = lax.psum(partial_value, "frame").astype(jnp.float32).astype(jnp.bfloat16)
    positions = jnp.arange(pixels, dtype=jnp.int32)
    row_pos = (positions // GRID_W).astype(jnp.float32) / (GRID_H - 1)
    col_pos = (positions % GRID_W).astype(jnp.float32) / (GRID_W - 1)
    blk = min(tr_dev, 64)
    blocks = tr_dev // blk
    grouped = queries.reshape(blocks, blk, chan)
    sampled_list, row_list, col_list = ([], [], [])
    maps = feature_maps[0]

    def per_block(qblock):
        return block_terms(qblock, maps, conv_weight, conv_bias, head_weight, row_pos, col_pos)

    sampled_f, row_f, col_f = lax.map(per_block, grouped)
    sampled_list.append(sampled_f.reshape(tr_dev, chan))
    row_list.append(row_f.reshape(tr_dev))
    col_list.append(col_f.reshape(tr_dev))
    sampled = jnp.stack(sampled_list, axis=1)
    row_est = jnp.stack(row_list, axis=1)
    col_est = jnp.stack(col_list, axis=1)
    rims = padded_2(sampled, (("frame", 1),), 1)
    projected = project(rims, mix_in)
    global_frame = frame_here * f_dev - 1 + jnp.arange(f_dev + 2, dtype=jnp.int32)
    valid = (global_frame >= 0) & (global_frame < frame_count * f_dev)
    extended = jnp.where(valid[None, :, None], projected, 0.0)
    delta = temporal_mix(extended, temporal_taps, mix_gain, mix_out)
    local_est = assemble(row_est, col_est, delta).reshape(frame_count, sub_rows, 3, f_dev)
    gathered = lax.all_to_all(local_est, "frame", split_axis=0, concat_axis=3, tiled=True)
    return gathered.reshape(sub_rows, 3, frame_count * f_dev)


def solution(mesh):
    placed = (
        P(("clip", "frame"), None, None),
        P("clip"),
        P("clip"),
        P("clip"),
        P("clip"),
        P(),
        P(),
        P(),
        P(),
        P(),
        P(),
        P(),
    )
    return jax.shard_map(
        on_device,
        mesh=mesh,
        in_specs=placed,
        out_specs=P(("clip", "frame", "track"), None, None),
        check_vma=False,
    )
```

profile of v0, /device:TPU:0, one launch (start us, length us, event | category | flops | bytes accessed | tf_op | source)
XLA Modules:
  0.0 403.0 jit_solution(6857952410239867091)
XLA Ops:
  6.8 1.6 gather_fusion
  8.4 1.6 gather_fusion.1
  10.1 1.6 gather_fusion.2
  11.7 1.6 gather_fusion.3
  13.4 2.6 gather_fusion.4
  16.8 37.1 %all-reduce.3.cloned.1.call-done = bf16[2,64,256]{2,1,0:T(8,128)(2,1)} async-done(((bf16[2,64,256]{2,1,0:T(8,128)(2,1)}), bf16[2,64,256]{2,1,0:T(8,128)(2,1)}) %all-reduce.3.cloned.1.call-update) | async-done | bytes 65552 | tf_op jit(solution)/shard_map/psum | solution.py:126
  53.9 322.9 %while.17 = (s32[]{:T(128)}, bf16[2,64,256]{2,1,0:T(8,128)(2,1)S(1)}, bf16[2,64]{1,0:T(2,128)(2,1)S(1)}, bf16[2,64]{1,0:T(2,128)(2,1)S(1)}, f32[16]{0:T(128)S(1)...) while((s32[]{:T(128)}, ...), condition=%wide.region_6.7_spmd.clone, body=%wide.region_1.6_spmd.clone.sunk | while | flops 359751424 | bytes 14882489 | solution.py:139
  54.7 0.7 fusion.91
  55.4 0.7 fusion.92
  56.1 0.7 fusion.93
  61.1 2.4 convolution_multiply_fusion.2
  63.5 2.2 reshape.346
  65.7 142.6 %fusion.97 = (f32[64]{0:T(128)S(1)}, f32[64,64,64]{2,1,0:T(8,128)S(1)}) fusion(f32[]{:T(128)} %bitcast.408, f32[]{:T(128)} %bitcast.409, f32[]{:T(128)} %bitcast.410, f32[]{:T(128)} %bitcast.411, f32[64,64,64]{2,1,0:T(8,128)} %reshape.346, f32[]{:T(128)} %bitcast.412, f32[]{:T(128)} %bitcast.413, f32[]{:T(128)} %bitcast.414, f32[]{:T(128)} %bitcast.415, ...), kind=kLoop, calls=%fused_computation.97.clone.1 | loop fusion | flops 88080320 | bytes 2098112 | tf_op jit(solution)/shard_map/while/body/eval_jaxpr/reduce_max | solution.py:48
  208.3 1.0 fusion.98
  209.5 1.8 multiply_reduce_fusion.4
  211.3 1.6 reshape.347
  212.9 2.4 fusion.99
  215.4 0.7 fusion.90
  216.1 0.7 fusion.91
  216.9 0.7 fusion.92
  217.6 0.7 fusion.93
  222.6 2.4 convolution_multiply_fusion.2
  225.0 2.2 reshape.346
  227.2 142.6 %fusion.97 = (f32[64]{0:T(128)S(1)}, f32[64,64,64]{2,1,0:T(8,128)S(1)}) fusion(f32[]{:T(128)} %bitcast.408, f32[]{:T(128)} %bitcast.409, f32[]{:T(128)} %bitcast.410, f32[]{:T(128)} %bitcast.411, f32[64,64,64]{2,1,0:T(8,128)} %reshape.346, f32[]{:T(128)} %bitcast.412, f32[]{:T(128)} %bitcast.413, f32[]{:T(128)} %bitcast.414, f32[]{:T(128)} %bitcast.415, ...), kind=kLoop, calls=%fused_computation.97.clone.1 | loop fusion | flops 88080320 | bytes 2098112 | tf_op jit(solution)/shard_map/while/body/eval_jaxpr/reduce_max | solution.py:48
  369.7 1.0 fusion.98
  370.9 1.8 multiply_reduce_fusion.4
  372.8 1.6 reshape.347
  374.4 2.4 fusion.99
  376.8 3.3 collective-permute-start
  380.2 1.3 collective-permute-start.1
  382.1 4.3 %collective-permute-done.1 = bf16[128,1,256]{2,0,1:T(8,128)(2,1)S(1)} collective-permute-done((bf16[128,1,256]{2,0,1:T(8,128)(2,1)S(1)}, bf16[128,1,256]{2,0,1:T(8,128)(2,1)S(1)}, u32[]{:S(2)}, u32[]{:S(2)}) %collective-permute-start.1) | collective-permute-done | bytes 65568 | tf_op jit(solution)/shard_map/ppermute | solution.py:19
  387.6 7.9 %all_to_all.15 = f32[4,32,3,1]{1,3,2,0:T(1,128)S(1)} all-to-all(f32[4,32,3,1]{1,3,2,0:T(1,128)S(1)} %copy.15), channel_id=1, replica_groups=mesh['clip'=2,'frame'=4,'track'=4] {'frame'}, dimensions={0} | all-to-all | bytes 3072 | tf_op jit(solution)/shard_map/all_to_all | solution.py:153
  (71 shorter events, 13.2 us)
Async XLA Ops:
  6.5 379.8 %copy-start = (bf16[256,1024]{1,0:T(8,128)(2,1)S(1)}, bf16[256,1024]{1,0:T(8,128)(2,1)}, u32[]{:S(2)}) copy-start(bf16[256,1024]{1,0:T(8,128)(2,1)} %param.22) | copy-start | bytes 1572868
  6.5 10.2 %copy-start.4 = (f32[3,1024]{1,0:T(4,128)S(1)}, f32[3,1024]{1,0:T(4,128)}, u32[]{:S(2)}) copy-start(f32[3,1024]{1,0:T(4,128)} %param.23) | copy-start | bytes 36868
  6.5 47.4 %copy-start.1 = (f32[16,9]{1,0:T(8,128)S(1)}, f32[16,9]{1,0:T(8,128)}, u32[]{:S(2)}) copy-start(f32[16,9]{1,0:T(8,128)} %param.19) | copy-start | bytes 1732
  6.5 47.4 %copy-start.3 = (f32[16]{0:T(128)S(1)}, f32[16]{0:T(128)}, u32[]{:S(2)}) copy-start(f32[16]{0:T(128)} %param.20) | copy-start | bytes 196
  6.5 47.4 %copy-start.2 = (f32[16]{0:T(128)S(1)}, f32[16]{0:T(128)}, u32[]{:S(2)}) copy-start(f32[16]{0:T(128)} %param.21) | copy-start | bytes 196
  6.5 47.4 %all-reduce.3.cloned.1.call-start = ((), (), s32[]{:S(2)}) async-start(), calls=%async_computation.1 | async-start | bytes 131072 | tf_op jit(solution)/shard_map/psum | solution.py:126
  376.8 5.2 %collective-permute-start = (bf16[128,1,256]{2,0,1:T(8,128)(2,1)S(1)}, bf16[128,1,256]{2,0,1:T(8,128)(2,1)S(1)}, u32[]{:S(2)}, u32[]{:S(2)}) collective-permute-start(bf16[128,1,256]{2,0,1:T(8,128)(2,1)S(1)} %bitcast.589), channel_id=1, source_target_pairs={{0,4},{4,8},{8,12},{1,5},{5,9},{9,13},{2,6},{6,10},{10,14},{3,7},{... | collective-permute-start | bytes 196616 | tf_op jit(solution)/shard_map/ppermute | solution.py:16
  380.2 6.2 %collective-permute-start.1 = (bf16[128,1,256]{2,0,1:T(8,128)(2,1)S(1)}, bf16[128,1,256]{2,0,1:T(8,128)(2,1)S(1)}, u32[]{:S(2)}, u32[]{:S(2)}) collective-permute-start(bf16[128,1,256]{2,0,1:T(8,128)(2,1)S(1)} %bitcast.590), channel_id=1, source_target_pairs={{4,0},{8,4},{12,8},{5,1},{9,5},{13,9},{6,2},{10,6},{14,10},{7,3},{... | collective-permute-start | bytes 196616 | tf_op jit(solution)/shard_map/ppermute | solution.py:19
  381.7 5.3 %copy-start.5 = (bf16[1024,3]{0,1:T(4,128)(2,1)S(1)}, bf16[1024,3]{0,1:T(4,128)(2,1)}, u32[]{:S(2)}) copy-start(bf16[1024,3]{0,1:T(4,128)(2,1)} %param.25) | copy-start | bytes 18436
  381.7 5.3 %copy-start.6 = (f32[1024]{0:T(1024)S(1)}, f32[1024]{0:T(1024)}, u32[]{:S(2)}) copy-start(f32[1024]{0:T(1024)} %param.24) | copy-start | bytes 12292
Sparse Core Ops, SparseCore 0:
  16.9 37.0 all-reduce.2
where the time goes:
time: 406 us; the launch traced here: 403 us
  other arithmetic  292 us (72%)
  waiting for transfers between devices  41.8 us (10%)
  local copies, waits for them, and re-layouts  32.8 us (8%)
  between operations  13.5 us (3%)
  matrix products  10.4 us (3%)
  blocking collectives  7.93 us (2%)
  starting transfers between devices  4.66 us (1%)
    reduce_max x2, other arithmetic, block_terms(): heat = jax.nn.softmax(logit.reshape(cost.shape), axis=-1)  285 us
    psum x1, waiting for transfers between devices, on_device(): lax.psum(partial_value, 'frame').astype(jnp.float32).astype(jnp.bfloat16)  37.1 us
    slice x16, local copies, waits for them, and re-layouts, conv_logits(): conv_weight[channel, tap]  11.5 us
  transfers between devices with their start and end apart: 3, of which 3 were waited for; matrix products, arithmetic and copies ran while one was open for 0% of the time, Pallas kernels for 0%

commit v1 on v0

--- a/solution.py
+++ b/solution.py
@@ -123,7 +123,11 @@
     flat = jnp.clip(local_frame, 0, f_dev - 1) * pixels + pixel_ids
     picks = feature_maps.reshape(f_dev * pixels, chan)[flat]
     partial_value = jnp.where(owned[:, None], picks, jnp.zeros((), picks.dtype))
-    queries = lax.psum(partial_value, "frame").astype(jnp.float32).astype(jnp.bfloat16)
+    queries = (
+        jnp.sum(lax.all_gather(partial_value, "frame"), axis=0)
+        .astype(jnp.float32)
+        .astype(jnp.bfloat16)
+    )
     positions = jnp.arange(pixels, dtype=jnp.int32)
     row_pos = (positions // GRID_W).astype(jnp.float32) / (GRID_H - 1)
     col_pos = (positions % GRID_W).astype(jnp.float32) / (GRID_W - 1)

time: 406 us -> 373 us (0.919)
  waiting for transfers between devices: 41.8 us -> 4.65 us
  blocking collectives: 7.93 us -> 24.8 us
  between operations: 13.5 us -> 0.19 us
    psum x1 -> x0, waiting for transfers between devices: 37.1 us -> none  [on_device(): lax.psum(partial_value, 'frame').astype(jnp.float32).astype(jnp.bfloat16)]
    all_gather x0 -> x1, blocking collectives: none -> 15.7 us  [on_device(): lax.all_gather(partial_value, 'frame')]
  transfers between devices with their start and end apart: 3 -> 2, of which waited for: 3 -> 2; matrix products, arithmetic and copies ran while one was open for 0% -> 0% of each run, Pallas kernels for 0% -> 0%
where the time goes in v1:
time: 373 us; the launch traced here: 369 us
  other arithmetic  291 us (78%)
  local copies, waits for them, and re-layouts  32.8 us (9%)
  blocking collectives  24.8 us (7%)
  matrix products  10.3 us (3%)
  starting transfers between devices  5.21 us (1%)
  waiting for transfers between devices  4.65 us (1%)
    reduce_max x2, other arithmetic, block_terms(): heat = jax.nn.softmax(logit.reshape(cost.shape), axis=-1)  285 us
    all_gather x1, blocking collectives, on_device(): lax.all_gather(partial_value, 'frame')  15.7 us
    slice x16, local copies, waits for them, and re-layouts, conv_logits(): conv_weight[channel, tap]  11.5 us
    all_to_all x1, blocking collectives, on_device(): lax.all_to_all(local_est, 'frame', split_axis=0, concat_axis=3, tiled=True)  9.1 us
  transfers between devices with their start and end apart: 2, of which 2 were waited for; matrix products, arithmetic and copies ran while one was open for 0% of the time, Pallas kernels for 0%

profile of v1, /device:TPU:0, one launch (start us, length us, event | category | flops | bytes accessed | tf_op | source)
XLA Modules:
  0.0 369.4 jit_solution(15781205720743745966)
XLA Ops:
  0.2 1.6 gather_fusion
  1.9 1.6 gather_fusion.1
  3.5 1.6 gather_fusion.2
  5.2 1.6 gather_fusion.3
  6.9 2.6 gather_fusion.4
  9.6 15.7 %all_gather.4 = bf16[4,128,256]{2,1,0:T(8,128)(2,1)S(1)} all-gather(bf16[1,128,256]{2,1,0:T(8,128)(2,1)S(1)} %bitcast_select_fusion), channel_id=1, replica_groups=mesh['clip'=2,'frame'=4,'track'=4] {'frame'}, dimensions={0}, use_global_device_ids=true | all-gather | bytes 327680 | tf_op jit(solution)/shard_map/all_gather | solution.py:127
  25.3 322.9 %while.17 = (s32[]{:T(128)}, bf16[2,64,256]{2,1,0:T(8,128)(2,1)S(1)}, bf16[2,64]{1,0:T(2,128)(2,1)S(1)}, bf16[2,64]{1,0:T(2,128)(2,1)S(1)}, f32[16]{0:T(128)S(1)...) while((s32[]{:T(128)}, ...), condition=%wide.region_6.7_spmd.clone, body=%wide.region_1.6_spmd.clone.sunk | while | flops 359751424 | bytes 14881981 | solution.py:143
  25.3 0.7 fusion.90
  26.1 0.7 fusion.91
  28.2 0.7 fusion.94
  29.0 0.7 fusion.95
  32.5 2.3 convolution_multiply_fusion.2
  34.9 2.2 reshape.372
  37.1 142.6 %fusion.97 = (f32[64]{0:T(128)S(1)}, f32[64,64,64]{2,1,0:T(8,128)S(1)}) fusion(f32[]{:T(128)} %bitcast.410, f32[]{:T(128)} %bitcast.411, f32[]{:T(128)} %bitcast.412, f32[]{:T(128)} %bitcast.413, f32[64,64,64]{2,1,0:T(8,128)} %reshape.372, f32[]{:T(128)} %bitcast.414, f32[]{:T(128)} %bitcast.415, f32[]{:T(128)} %bitcast.416, f32[]{:T(128)} %bitcast.417, ...), kind=kLoop, calls=%fused_computation.97.clone.1 | loop fusion | flops 88080320 | bytes 2098112 | tf_op jit(solution)/shard_map/while/body/eval_jaxpr/reduce_max | solution.py:48
  179.7 1.0 fusion.98
  180.9 1.8 multiply_reduce_fusion.4
  182.7 1.6 reshape.373
  184.4 2.4 fusion.99
  186.8 0.7 fusion.90
  187.5 0.7 fusion.91
  190.4 0.7 fusion.95
  194.0 2.3 convolution_multiply_fusion.2
  196.4 2.2 reshape.372
  198.5 142.6 %fusion.97 = (f32[64]{0:T(128)S(1)}, f32[64,64,64]{2,1,0:T(8,128)S(1)}) fusion(f32[]{:T(128)} %bitcast.410, f32[]{:T(128)} %bitcast.411, f32[]{:T(128)} %bitcast.412, f32[]{:T(128)} %bitcast.413, f32[64,64,64]{2,1,0:T(8,128)} %reshape.372, f32[]{:T(128)} %bitcast.414, f32[]{:T(128)} %bitcast.415, f32[]{:T(128)} %bitcast.416, f32[]{:T(128)} %bitcast.417, ...), kind=kLoop, calls=%fused_computation.97.clone.1 | loop fusion | flops 88080320 | bytes 2098112 | tf_op jit(solution)/shard_map/while/body/eval_jaxpr/reduce_max | solution.py:48
  341.2 1.0 fusion.98
  342.3 1.8 multiply_reduce_fusion.4
  344.2 1.6 reshape.373
  345.8 2.4 fusion.99
  348.3 3.9 %collective-permute-start = (bf16[128,1,256]{2,0,1:T(8,128)(2,1)S(1)}, bf16[128,1,256]{2,0,1:T(8,128)(2,1)S(1)}, u32[]{:S(2)}, u32[]{:S(2)}) collective-permute-start(bf16[128,1,256]{2,0,1:T(8,128)(2,1)S(1)} %bitcast.591), channel_id=1, source_target_pairs={{0,4},{4,8},{8,12},{1,5},{5,9},{9,13},{2,6},{6,10},{10,14},{3,7},{... | collective-permute-start | bytes 196616 | tf_op jit(solution)/shard_map/ppermute | solution.py:16
  352.2 1.3 collective-permute-start.1
  354.1 4.3 %collective-permute-done.1 = bf16[128,1,256]{2,0,1:T(8,128)(2,1)S(1)} collective-permute-done((bf16[128,1,256]{2,0,1:T(8,128)(2,1)S(1)}, bf16[128,1,256]{2,0,1:T(8,128)(2,1)S(1)}, u32[]{:S(2)}, u32[]{:S(2)}) %collective-permute-start.1) | collective-permute-done | bytes 65568 | tf_op jit(solution)/shard_map/ppermute | solution.py:19
  359.7 9.1 %all_to_all.15 = f32[4,32,3,1]{1,3,2,0:T(1,128)S(1)} all-to-all(f32[4,32,3,1]{1,3,2,0:T(1,128)S(1)} %copy.15), channel_id=1, replica_groups=mesh['clip'=2,'frame'=4,'track'=4] {'frame'}, dimensions={0} | all-to-all | bytes 3072 | tf_op jit(solution)/shard_map/all_to_all | solution.py:157
  (70 shorter events, 12.5 us)
Async XLA Ops:
  0.0 358.4 %copy-start = (bf16[256,1024]{1,0:T(8,128)(2,1)S(1)}, bf16[256,1024]{1,0:T(8,128)(2,1)}, u32[]{:S(2)}) copy-start(bf16[256,1024]{1,0:T(8,128)(2,1)} %param.22) | copy-start | bytes 1572868
  0.0 25.3 %copy-start.1 = (f32[16,9]{1,0:T(8,128)S(1)}, f32[16,9]{1,0:T(8,128)}, u32[]{:S(2)}) copy-start(f32[16,9]{1,0:T(8,128)} %param.19) | copy-start | bytes 1732
  0.0 25.3 %copy-start.3 = (f32[16]{0:T(128)S(1)}, f32[16]{0:T(128)}, u32[]{:S(2)}) copy-start(f32[16]{0:T(128)} %param.20) | copy-start | bytes 196
  0.0 25.3 %copy-start.2 = (f32[16]{0:T(128)S(1)}, f32[16]{0:T(128)}, u32[]{:S(2)}) copy-start(f32[16]{0:T(128)} %param.21) | copy-start | bytes 196
  25.3 328.2 %copy-start.4 = (f32[3,1024]{1,0:T(4,128)S(1)}, f32[3,1024]{1,0:T(4,128)}, u32[]{:S(2)}) copy-start(f32[3,1024]{1,0:T(4,128)} %param.23) | copy-start | bytes 36868
  348.3 5.8 %collective-permute-start = (bf16[128,1,256]{2,0,1:T(8,128)(2,1)S(1)}, bf16[128,1,256]{2,0,1:T(8,128)(2,1)S(1)}, u32[]{:S(2)}, u32[]{:S(2)}) collective-permute-start(bf16[128,1,256]{2,0,1:T(8,128)(2,1)S(1)} %bitcast.591), channel_id=1, source_target_pairs={{0,4},{4,8},{8,12},{1,5},{5,9},{9,13},{2,6},{6,10},{10,14},{3,7},{... | collective-permute-start | bytes 196616 | tf_op jit(solution)/shard_map/ppermute | solution.py:16
  352.2 6.2 %collective-permute-start.1 = (bf16[128,1,256]{2,0,1:T(8,128)(2,1)S(1)}, bf16[128,1,256]{2,0,1:T(8,128)(2,1)S(1)}, u32[]{:S(2)}, u32[]{:S(2)}) collective-permute-start(bf16[128,1,256]{2,0,1:T(8,128)(2,1)S(1)} %bitcast.592), channel_id=1, source_target_pairs={{4,0},{8,4},{12,8},{5,1},{9,5},{13,9},{6,2},{10,6},{14,10},{7,3},{... | collective-permute-start | bytes 196616 | tf_op jit(solution)/shard_map/ppermute | solution.py:19
  353.7 5.3 %copy-start.5 = (bf16[1024,3]{0,1:T(4,128)(2,1)S(1)}, bf16[1024,3]{0,1:T(4,128)(2,1)}, u32[]{:S(2)}) copy-start(bf16[1024,3]{0,1:T(4,128)(2,1)} %param.25) | copy-start | bytes 18436
  353.7 5.3 %copy-start.6 = (f32[1024]{0:T(1024)S(1)}, f32[1024]{0:T(1024)}, u32[]{:S(2)}) copy-start(f32[1024]{0:T(1024)} %param.24) | copy-start | bytes 12292
